TPU v7x, 512 devices: a whole 4x4x16 slice. The times are simulated.
512 devices in a mesh: seq: 64 (over y, z_lo, core), strand: 2 (over z_hi), head: 4 (over x).
Axes of the slice: x: 4, y: 4, z: 16 (z_hi: 2, z_lo: 8; z = z_hi * 8 + z_lo), core: 2. Of those that a mesh axis runs over, the one named last changes fastest.
Arguments:
- top: bfloat16 [4, 2, 16384, 1536], P('head', 'strand', 'seq'), may hold values from -6 to 6
- grad_heads: bfloat16 [4, 2, 16384, 1536], P(None, 'strand', 'seq', 'head'), may hold values from -6 to 6
- tap_weight_grid: bfloat16 [3, 768, 768], P(None, 'seq'), may hold values from -0.125 to 0.125
- out_w: bfloat16 [768, 768], P('seq'), may hold values from -0.21875 to 0.21875
- mix_w: bfloat16 [768, 768], P('seq'), may hold values from -0.21875 to 0.21875
- rc_perm: int32 [768], replicated, may hold values from 0 to 767, each once
Outputs:
- restored: bfloat16 [4, 2, 16384, 1536], P('head', 'strand', 'seq')
- grad_input: bfloat16 [4, 2, 16384, 1536], P('head', 'strand', 'seq')
Inputs may be any that keep to these rules, and one draw needn't show every extreme that they name: `rc_perm`: every channel index appears exactly once.
All inputs are finite; a program needn't handle non-finite values.
Results may differ from a plain program's by a relative error of at most 0.008.
Values may be sent and summed in bfloat16 or wider, within the bound.
No kernel may reach another device: no remote copies, remote signals or barrier semaphores. Data moves between devices by JAX's collectives and lax.ppermute only.
A program may use at most 64 MiB of HBM per device.

v0:
```python
import jax
import jax.numpy as jnp
from jax import lax
from jax.sharding import PartitionSpec as P


def rows_first(arrays, axis, dims):
    turned = [jnp.moveaxis(a, dim, 0) for a, dim in zip(arrays, dims)]
    widths = [t[0].size for t in turned]
    both = jnp.concatenate([t.reshape(-1, w) for t, w in zip(turned, widths)], axis=1)
    result = lax.all_gather(both, axis, axis=0, tiled=True)
    pieces = jnp.split(result, [sum(widths[:k]) for k in range(1, len(widths))], axis=1)
    return tuple(
        (
            jnp.moveaxis(b.reshape(-1, *t.shape[1:]), 0, dim)
            for b, t, dim in zip(pieces, turned, dims)
        )
    )


def swapped(value, axis, bit):
    mask = 2**bit
    pairs = [(source, source ^ mask) for source in range(lax.axis_size(axis))]
    return lax.ppermute(value, axis, pairs)


def with_halo(array, sides, width):
    for axis, dim in sides:
        devices, length = (lax.axis_size(axis), array.shape[dim])
        up = [(i, (i + 1) % devices) for i in range(devices - 1)]
        down = [(j, i) for i, j in up]
        last = lax.slice_in_dim(array, length - width, length, axis=dim)
        first = lax.slice_in_dim(array, 0, width, axis=dim)
        before = lax.ppermute(last, axis, up)
        after = lax.ppermute(first, axis, down)
        array = jnp.concatenate([before, array, after], axis=dim)
    return array


def taps_forward(padded, kernel, length, dilation):
    total = jnp.dot(padded[0:length], kernel[0], preferred_element_type=jnp.float32)
    total = total + jnp.dot(
        padded[dilation : dilation + length], kernel[1], preferred_element_type=jnp.float32
    )
    return total + jnp.dot(
        padded[2 * dilation : 2 * dilation + length], kernel[2], preferred_element_type=jnp.float32
    )


def taps_backward(padded, kernel, length, dilation):
    total = jnp.einsum(
        "pd,cd->pc",
        padded[2 * dilation : 2 * dilation + length],
        kernel[0],
        preferred_element_type=jnp.float32,
    )
    total = total + jnp.einsum(
        "pd,cd->pc",
        padded[dilation : dilation + length],
        kernel[1],
        preferred_element_type=jnp.float32,
    )
    return total + jnp.einsum(
        "pd,cd->pc", padded[0:length], kernel[2], preferred_element_type=jnp.float32
    )


def shards(top, grad_heads, tap_weight_grid, out_w, mix_w, rc_perm):
    length = top.shape[2]
    dilation = length // 2
    half = top.shape[3] // 2
    cotan = lax.all_to_all(grad_heads, "head", split_axis=0, concat_axis=3, tiled=True)[0, 0]
    conv_full, out_full, mix_full = rows_first((tap_weight_grid, out_w, mix_w), "seq", (1, 0, 0))
    top_a = top[0, 0, :, :half]
    top_b = top[0, 0, :, half:]
    grad_a = cotan[:, :half]
    second_gradient = cotan[:, half:]
    inverse = jnp.zeros((half,), jnp.int32).at[rc_perm].set(jnp.arange(half, dtype=jnp.int32))
    other_a = swapped(top_a, "strand", 0)
    mirror = jnp.take(other_a, rc_perm, axis=1)
    paired = (top_a.astype(jnp.float32) + mirror.astype(jnp.float32)).astype(jnp.bfloat16)
    mixing = jnp.dot(paired, mix_full, preferred_element_type=jnp.float32)
    second_input = (top_b.astype(jnp.float32) - mixing).astype(jnp.bfloat16)
    padded_b = with_halo(second_input, (("seq", 0),), dilation)
    preactivation_rows = taps_forward(padded_b, conv_full, length, dilation)
    hidden = jax.nn.gelu(preactivation_rows).astype(jnp.bfloat16)
    branch_out = jnp.dot(hidden, out_full, preferred_element_type=jnp.float32)
    input_a = (top_a.astype(jnp.float32) - branch_out).astype(jnp.bfloat16)
    backed = jnp.einsum(
        "pd,cd->pc", second_gradient, mix_full, preferred_element_type=jnp.float32
    ).astype(jnp.bfloat16)
    returned = swapped(jnp.take(backed, inverse, axis=1), "strand", 0)
    cot_a = (
        grad_a.astype(jnp.float32) + backed.astype(jnp.float32) + returned.astype(jnp.float32)
    ).astype(jnp.bfloat16)
    pulled = jnp.einsum("pd,cd->pc", cot_a, out_full, preferred_element_type=jnp.float32)
    unused, slope = jax.vjp(jax.nn.gelu, preactivation_rows)
    preactivation_cotangent = slope(pulled)[0].astype(jnp.bfloat16)
    padded_cot = with_halo(preactivation_cotangent, (("seq", 0),), dilation)
    cotangent_second = (
        second_gradient.astype(jnp.float32) + taps_backward(padded_cot, conv_full, length, dilation)
    ).astype(jnp.bfloat16)
    restored = jnp.concatenate([input_a, second_input], axis=1)[None, None]
    grad_input = jnp.concatenate([cot_a, cotangent_second], axis=1)[None, None]
    return (restored, grad_input)


def solution(mesh):
    placed = (
        P("head", "strand", "seq", None),
        P(None, "strand", "seq", "head"),
        P(None, "seq", None),
        P("seq", None),
        P("seq", None),
        P(),
    )
    return jax.shard_map(
        shards,
        mesh=mesh,
        in_specs=placed,
        out_specs=(P("head", "strand", "seq", None), P("head", "strand", "seq", None)),
        check_vma=False,
    )
```

profile of v0, /device:TPU:111, one launch (start us, length us, event | category | flops | bytes accessed | tf_op | source)
XLA Modules:
  0.0 258.7 jit_solution(8820897414289662014)
XLA Ops:
  8.2 1.4 maximum_bitcast_fusion.2
  10.7 12.7 %collective-permute-start = (bf16[256,768]{1,0:T(8,128)(2,1)S(1)}, bf16[256,768]{1,0:T(8,128)(2,1)S(1)}, u32[]{:S(2)}, u32[]{:S(2)}) collective-permute-start(bf16[256,768]{1,0:T(8,128)(2,1)S(1)} %slice_bitcast_fusion.9), channel_id=1, source_target_pairs={{0,4},{4,0},{1,5},{5,1},{2,6},{6,2},{3,7},{7,3},{8,12},{12,8},{9,1... | collective-permute-start | bytes 1179656 | tf_op jit(solution)/shard_map/ppermute | solution.py:24
  23.4 4.2 %all-to-all-start = ((bf16[4,1,256,384]{3,2,1,0:T(8,128)(2,1)}), bf16[4,1,256,384]{3,2,1,0:T(8,128)(2,1)S(1)}, u32[]{:S(2)}, u32[]{:S(2)}) async-start(bf16[4,1,256,384]{3,2,1,0:T(8,128)(2,1)} %param.9), calls=%async_computation | async-start | bytes 1572864 | tf_op jit(solution)/shard_map/all_to_all | solution.py:72
  27.7 3.4 %scatter_custom_fusion = s32[768]{0:T(1024)S(1)} fusion(s32[768]{0:T(1024)S(1)} %compare_select_fusion.1, s32[768]{0:T(1024)S(1)} %iota.3, s32[]{:T(128)} %constant.9.clone.1), kind=kCustom, calls=%fused_computation.68 | custom fusion | bytes 3076 | tf_op jit(solution)/shard_map/scatter | solution.py:78
  31.1 16.4 %collective-permute-done = bf16[256,768]{1,0:T(8,128)(2,1)S(1)} collective-permute-done((bf16[256,768]{1,0:T(8,128)(2,1)S(1)}, bf16[256,768]{1,0:T(8,128)(2,1)S(1)}, u32[]{:S(2)}, u32[]{:S(2)}) %collective-permute-start) | collective-permute-done | bytes 393248 | tf_op jit(solution)/shard_map/ppermute | solution.py:24
  47.7 2.7 %gather_fusion = bf16[768,256]{1,0:T(8,128)(2,1)S(1)} fusion(bf16[256,768]{0,1:T(8,128)(2,1)S(1)} %copy.27, s32[1024]{0:T(1024)S(1)} %pad_clamp_fusion.1), kind=kCustom, calls=%fused_computation.clone | custom fusion | bytes 789504 | tf_op jit(solution)/shard_map/jit(_take)/gather | solution.py:80
  51.3 1.2 copy.34
  52.4 111.7 %all-gather.3.cloned.1.call-done = bf16[64,12,3840]{2,1,0:T(8,128)(2,1)} async-done(((bf16[1,12,3840]{2,1,0:T(8,128)(2,1)}), bf16[64,12,3840]{2,1,0:T(8,128)(2,1)}) %all-gather.3.cloned.1.call-update) | async-done | bytes 5898256 | tf_op jit(solution)/shard_map/all_gather | solution.py:11
  164.1 9.6 %reshape.49 = bf16[768,3840]{1,0:T(8,128)(2,1)} reshape(bf16[64,12,3840]{2,1,0:T(8,128)(2,1)} %all-gather.3.cloned.1.call-done) | data formatting | bytes 11796480
  173.7 2.0 slice-done.2
  175.7 3.6 %copy.30 = bf16[768,2304]{0,1:T(8,128)(2,1)} copy(bf16[768,2304]{1,0:T(8,128)(2,1)S(1)} %slice-done.2) | data formatting | bytes 7077888 | tf_op jit(solution)/shard_map/split | solution.py:12
  179.3 2.2 fusion.3
  181.5 2.2 collective-permute-start.2
  183.7 4.6 %collective-permute-start.1 = (bf16[128,768]{1,0:T(8,128)(2,1)S(1)}, bf16[128,768]{1,0:T(8,128)(2,1)S(1)}, u32[]{:S(2)}, u32[]{:S(2)}) collective-permute-start(bf16[128,768]{1,0:T(8,128)(2,1)S(1)} %get-tuple-element.11), channel_id=1, source_target_pairs={{0,8},{8,16},{16,24},{24,32},{32,40},{40,48},{48,56},{56,64},{64,7... | collective-permute-start | bytes 589832 | tf_op jit(solution)/shard_map/ppermute | solution.py:34
  188.3 1.7 fusion.6
  190.0 2.7 %gather_fusion.1 = bf16[768,256]{1,0:T(8,128)(2,1)S(1)} fusion(bf16[256,768]{0,1:T(8,128)(2,1)S(1)} %fusion.6, s32[1024]{0:T(1024)S(1)} %pad_clamp_fusion), kind=kCustom, calls=%fused_computation.1.clone | custom fusion | bytes 789504 | tf_op jit(solution)/shard_map/jit(_take)/gather | solution.py:92
  192.9 2.5 collective-permute-start.3
  195.4 1.9 fusion.8
  197.3 1.8 fusion.10
  200.2 2.3 fusion.4
  203.4 32.8 %collective-permute-done.3 = bf16[256,768]{0,1:T(8,128)(2,1)S(1)} collective-permute-done((bf16[256,768]{0,1:T(8,128)(2,1)S(1)}, bf16[256,768]{0,1:T(8,128)(2,1)S(1)}, u32[]{:S(2)}, u32[]{:S(2)}) %collective-permute-start.3) | collective-permute-done | bytes 393248 | tf_op jit(solution)/shard_map/ppermute | solution.py:24
  237.2 4.6 %collective-permute-start.5 = (bf16[128,768]{1,0:T(8,128)(2,1)S(1)}, bf16[128,768]{1,0:T(8,128)(2,1)S(1)}, u32[]{:S(2)}, u32[]{:S(2)}) collective-permute-start(bf16[128,768]{1,0:T(8,128)(2,1)S(1)} %get-tuple-element.10), channel_id=1, source_target_pairs={{0,8},{8,16},{16,24},{24,32},{32,40},{40,48},{48,56},{56,64},{64,7... | collective-permute-start | bytes 589832 | tf_op jit(solution)/shard_map/ppermute | solution.py:34
  241.8 1.9 collective-permute-start.4
  245.0 5.0 %collective-permute-done.4 = bf16[128,768]{1,0:T(8,128)(2,1)S(1)} collective-permute-done((bf16[128,768]{1,0:T(8,128)(2,1)S(1)}, bf16[128,768]{1,0:T(8,128)(2,1)S(1)}, u32[]{:S(2)}, u32[]{:S(2)}) %collective-permute-start.4) | collective-permute-done | bytes 196640 | tf_op jit(solution)/shard_map/ppermute | solution.py:35
  (45 shorter events, 9.5 us)
Async XLA Ops:
  7.2 157.0 %all-gather.3.cloned.1.call-start = ((), (), s32[]{:S(2)}) async-start(), calls=%async_computation.1 | async-start | bytes 7987200 | tf_op jit(solution)/shard_map/all_gather | solution.py:11
  8.1 19.5 %copy-start.3 = (s32[768]{0:T(1024)S(1)}, s32[768]{0:T(1024)}, u32[]{:S(2)}) copy-start(s32[768]{0:T(1024)} %param.13) | copy-start | bytes 9220
  10.7 36.8 %collective-permute-start = (bf16[256,768]{1,0:T(8,128)(2,1)S(1)}, bf16[256,768]{1,0:T(8,128)(2,1)S(1)}, u32[]{:S(2)}, u32[]{:S(2)}) collective-permute-start(bf16[256,768]{1,0:T(8,128)(2,1)S(1)} %slice_bitcast_fusion.9), channel_id=1, source_target_pairs={{0,4},{4,0},{1,5},{5,1},{2,6},{6,2},{3,7},{7,3},{8,12},{12,8},{9,1... | collective-permute-start | bytes 1179656 | tf_op jit(solution)/shard_map/ppermute | solution.py:24
  23.4 27.8 %all-to-all-start = ((bf16[4,1,256,384]{3,2,1,0:T(8,128)(2,1)}), bf16[4,1,256,384]{3,2,1,0:T(8,128)(2,1)S(1)}, u32[]{:S(2)}, u32[]{:S(2)}) async-start(bf16[4,1,256,384]{3,2,1,0:T(8,128)(2,1)} %param.9), calls=%async_computation | async-start | bytes 1572864 | tf_op jit(solution)/shard_map/all_to_all | solution.py:72
  173.7 2.0 slice-start.2
  179.3 9.0 %copy-start.1 = (bf16[1,1,256,4,384]{2,4,3,1,0:T(8,128)(2,1)S(1)}, bf16[1,1,256,4,384]{2,4,3,1,0:T(8,128)(2,1)}, u32[]{:S(2)}) copy-start(bf16[1,1,256,4,384]{2,4,3,1,0:T(8,128)(2,1)} %copy.34) | copy-start | bytes 2359300
  181.5 15.8 %collective-permute-start.2 = (bf16[128,768]{1,0:T(8,128)(2,1)S(1)}, bf16[128,768]{1,0:T(8,128)(2,1)S(1)}, u32[]{:S(2)}, u32[]{:S(2)}) collective-permute-start(bf16[128,768]{1,0:T(8,128)(2,1)S(1)} %get-tuple-element.12), channel_id=1, source_target_pairs={{8,0},{16,8},{24,16},{32,24},{40,32},{48,40},{56,48},{64,56},{72,6... | collective-permute-start | bytes 589832 | tf_op jit(solution)/shard_map/ppermute | solution.py:35
  183.7 15.4 %collective-permute-start.1 = (bf16[128,768]{1,0:T(8,128)(2,1)S(1)}, bf16[128,768]{1,0:T(8,128)(2,1)S(1)}, u32[]{:S(2)}, u32[]{:S(2)}) collective-permute-start(bf16[128,768]{1,0:T(8,128)(2,1)S(1)} %get-tuple-element.11), channel_id=1, source_target_pairs={{0,8},{8,16},{16,24},{24,32},{32,40},{40,48},{48,56},{56,64},{64,7... | collective-permute-start | bytes 589832 | tf_op jit(solution)/shard_map/ppermute | solution.py:34
  192.9 43.3 %collective-permute-start.3 = (bf16[256,768]{0,1:T(8,128)(2,1)S(1)}, bf16[256,768]{0,1:T(8,128)(2,1)S(1)}, u32[]{:S(2)}, u32[]{:S(2)}) collective-permute-start(bf16[256,768]{0,1:T(8,128)(2,1)S(1)} %select_bitcast_fusion), channel_id=1, source_target_pairs={{0,4},{4,0},{1,5},{5,1},{2,6},{6,2},{3,7},{7,3},{8,12},{12,8},{9,1... | collective-permute-start | bytes 1179656 | tf_op jit(solution)/shard_map/ppermute | solution.py:24
  195.4 3.8 %copy-start = (bf16[768,2304]{0,1:T(8,128)(2,1)S(1)}, bf16[768,2304]{0,1:T(8,128)(2,1)}, u32[]{:S(2)}) copy-start(bf16[768,2304]{0,1:T(8,128)(2,1)} %copy.30) | copy-start | bytes 10616836
  199.1 1.1 copy-start.2
  199.1 37.2 %slice-start = ((s8[5898240]{0:T(1024)(128)(4,1)}), s8[4194304]{0:T(1024)(128)(4,1)S(1)}, s32[]{:S(2)}) async-start(s8[5898240]{0:T(1024)(128)(4,1)} %bitcast.63), calls=%async_computation.2 | async-start | bytes 8388608
  200.2 36.1 %slice-start.1 = ((s8[5898240]{0:T(1024)(128)(4,1)}), s8[1703936]{0:T(1024)(128)(4,1)S(1)}, s32[]{:S(2)}) async-start(s8[5898240]{0:T(1024)(128)(4,1)} %bitcast.63), calls=%async_computation.3 | async-start | bytes 3407872
  237.2 7.2 %collective-permute-start.5 = (bf16[128,768]{1,0:T(8,128)(2,1)S(1)}, bf16[128,768]{1,0:T(8,128)(2,1)S(1)}, u32[]{:S(2)}, u32[]{:S(2)}) collective-permute-start(bf16[128,768]{1,0:T(8,128)(2,1)S(1)} %get-tuple-element.10), channel_id=1, source_target_pairs={{0,8},{8,16},{16,24},{24,32},{32,40},{40,48},{48,56},{56,64},{64,7... | collective-permute-start | bytes 589832 | tf_op jit(solution)/shard_map/ppermute | solution.py:34
  241.8 8.2 %collective-permute-start.4 = (bf16[128,768]{1,0:T(8,128)(2,1)S(1)}, bf16[128,768]{1,0:T(8,128)(2,1)S(1)}, u32[]{:S(2)}, u32[]{:S(2)}) collective-permute-start(bf16[128,768]{1,0:T(8,128)(2,1)S(1)} %get-tuple-element.9), channel_id=1, source_target_pairs={{8,0},{16,8},{24,16},{32,24},{40,32},{48,40},{56,48},{64,56},{72,6... | collective-permute-start | bytes 589832 | tf_op jit(solution)/shard_map/ppermute | solution.py:35
Sparse Core Ops, SparseCore 0:
  10.1 153.9 all-gather.2
where the time goes:
time: 259 us
  waiting for transfers between devices  166 us (64%)
  starting transfers between devices  32.8 us (13%)
  local copies, waits for them, and re-layouts  29.9 us (12%)
  between operations  14.4 us (6%)
  matrix products  13 us (5%)
  other arithmetic  2.79 us (1%)
    all_gather x1, waiting for transfers between devices, rows_first(): result = lax.all_gather(both, axis, axis=0, tiled=True)  112 us
    ppermute x2, waiting for transfers between devices, swapped(): return lax.ppermute(value, axis, pairs)  49.1 us
    ppermute x2, starting transfers between devices, swapped(): return lax.ppermute(value, axis, pairs)  15.2 us
    unnamed x16, local copies, waits for them, and re-layouts  11.4 us
    ppermute x2, starting transfers between devices, with_halo(): before = lax.ppermute(last, axis, up)  9.16 us
    split x3, local copies, waits for them, and re-layouts, rows_first(): jnp.split(result, [sum(widths[:k]) for k in range(1, len(widths))], axis=1)  5.56 us
  transfers between devices with their start and end apart: 8, of which 5 were waited for; matrix products, arithmetic and copies ran while one was open for 9% of the time, Pallas kernels for 0%

commit v1 on v0

--- a/solution.py
+++ b/solution.py
@@ -8,7 +8,9 @@
     turned = [jnp.moveaxis(a, dim, 0) for a, dim in zip(arrays, dims)]
     widths = [t[0].size for t in turned]
     both = jnp.concatenate([t.reshape(-1, w) for t, w in zip(turned, widths)], axis=1)
-    result = lax.all_gather(both, axis, axis=0, tiled=True)
+    result = jnp.concatenate(
+        lax.all_to_all(jnp.stack([both] * lax.axis_size(axis)), axis, 0, 0), axis=0
+    )
     pieces = jnp.split(result, [sum(widths[:k]) for k in range(1, len(widths))], axis=1)
     return tuple(
         (

time: 259 us -> 505 us (1.95)
  the two profiles are of different devices: /device:TPU:111 before, /device:TPU:1 now
where the time goes in v1:
time: 505 us; the launch traced here: 504 us
  waiting for transfers between devices  391 us (77%)
  starting transfers between devices  64.9 us (13%)
  local copies, waits for them, and re-layouts  34.1 us (7%)
  matrix products  11.5 us (2%)
    all_to_all x1, waiting for transfers between devices, rows_first(): lax.all_to_all(jnp.stack([both] * lax.axis_size(axis)), axis, 0, 0)  200 us
    ppermute x2, waiting for transfers between devices, swapped(): return lax.ppermute(value, axis, pairs)  179 us
    all_to_all x1, starting transfers between devices, rows_first(): lax.all_to_all(jnp.stack([both] * lax.axis_size(axis)), axis, 0, 0)  20.9 us
    ppermute x2, starting transfers between devices, with_halo(): before = lax.ppermute(last, axis, up)  19.3 us
    ppermute x2, starting transfers between devices, swapped(): return lax.ppermute(value, axis, pairs)  15.9 us
  transfers between devices with their start and end apart: 8, of which 6 were waited for; matrix products, arithmetic and copies ran while one was open for 5% of the time, Pallas kernels for 0%

profile of v1, /device:TPU:1, one launch (start us, length us, event | category | flops | bytes accessed | tf_op | source)
XLA Modules:
  0.0 504.1 jit_solution(2632544550579318873)
XLA Ops:
  0.7 5.0 all-to-all-start.1
  5.8 8.2 %all-to-all-done.1 = bf16[4,1,256,384]{3,2,1,0:T(8,128)(2,1)S(1)} async-done(((bf16[4,1,256,384]{3,2,1,0:T(8,128)(2,1)}), bf16[4,1,256,384]{3,2,1,0:T(8,128)(2,1)S(1)}, u32[]{:S(2)}, u32[]{:S(2)}) %all-to-all-start.1) | async-done | bytes 786464 | tf_op jit(solution)/shard_map/all_to_all | solution.py:74
  14.0 3.6 stack.2
  17.6 20.9 %all-to-all-start = ((bf16[64,12,3840]{2,1,0:T(8,128)(2,1)}), bf16[64,12,3840]{2,1,0:T(8,128)(2,1)}, u32[]{:S(2)}, u32[]{:S(2)}) async-start(bf16[64,12,3840]{2,1,0:T(8,128)(2,1)} %stack.2), calls=%async_computation | async-start | bytes 15728640 | tf_op jit(solution)/shard_map/all_to_all | solution.py:12
  38.6 7.9 %collective-permute-start = (bf16[256,768]{1,0:T(8,128)(2,1)S(1)}, bf16[256,768]{1,0:T(8,128)(2,1)S(1)}, u32[]{:S(2)}, u32[]{:S(2)}) collective-permute-start(bf16[256,768]{1,0:T(8,128)(2,1)S(1)} %slice_bitcast_fusion.9), channel_id=1, source_target_pairs={{0,4},{4,0},{1,5},{5,1},{2,6},{6,2},{3,7},{7,3},{8,12},{12,8},{9,1... | collective-permute-start | bytes 1179656 | tf_op jit(solution)/shard_map/ppermute | solution.py:26
  46.6 3.4 scatter_custom_fusion
  50.0 160.4 %collective-permute-done = bf16[256,768]{1,0:T(8,128)(2,1)S(1)} collective-permute-done((bf16[256,768]{1,0:T(8,128)(2,1)S(1)}, bf16[256,768]{1,0:T(8,128)(2,1)S(1)}, u32[]{:S(2)}, u32[]{:S(2)}) %collective-permute-start) | collective-permute-done | bytes 393248 | tf_op jit(solution)/shard_map/ppermute | solution.py:26
  210.6 2.7 gather_fusion
  215.3 200.5 %all-to-all-done = bf16[64,12,3840]{2,1,0:T(8,128)(2,1)} async-done(((bf16[64,12,3840]{2,1,0:T(8,128)(2,1)}), bf16[64,12,3840]{2,1,0:T(8,128)(2,1)}, u32[]{:S(2)}, u32[]{:S(2)}) %all-to-all-start) | async-done | bytes 5898272 | tf_op jit(solution)/shard_map/all_to_all | solution.py:12
  415.8 9.6 %reshape.24 = bf16[768,3840]{1,0:T(8,128)(2,1)} reshape(bf16[64,12,3840]{2,1,0:T(8,128)(2,1)} %all-to-all-done) | data formatting | bytes 11796480 | tf_op jit(solution)/shard_map/reshape | solution.py:11
  425.4 2.7 copy-done.1
  430.3 1.9 collective-permute-start.2
  432.3 3.6 copy.18
  435.9 3.6 collective-permute-start.1
  439.5 1.8 fusion.6
  441.4 2.7 gather_fusion.1
  444.2 8.0 %collective-permute-start.3 = (bf16[256,768]{0,1:T(8,128)(2,1)S(1)}, bf16[256,768]{0,1:T(8,128)(2,1)S(1)}, u32[]{:S(2)}, u32[]{:S(2)}) collective-permute-start(bf16[256,768]{0,1:T(8,128)(2,1)S(1)} %select_bitcast_fusion), channel_id=1, source_target_pairs={{0,4},{4,0},{1,5},{5,1},{2,6},{6,2},{3,7},{7,3},{8,12},{12,8},{9,1... | collective-permute-start | bytes 1179656 | tf_op jit(solution)/shard_map/ppermute | solution.py:26
  452.2 1.9 fusion.8
  454.1 1.9 fusion.10
  457.2 2.3 fusion.4
  460.4 18.2 %collective-permute-done.3 = bf16[256,768]{0,1:T(8,128)(2,1)S(1)} collective-permute-done((bf16[256,768]{0,1:T(8,128)(2,1)S(1)}, bf16[256,768]{0,1:T(8,128)(2,1)S(1)}, u32[]{:S(2)}, u32[]{:S(2)}) %collective-permute-start.3) | collective-permute-done | bytes 393248 | tf_op jit(solution)/shard_map/ppermute | solution.py:26
  479.6 15.7 %collective-permute-start.5 = (bf16[128,768]{1,0:T(8,128)(2,1)S(1)}, bf16[128,768]{1,0:T(8,128)(2,1)S(1)}, u32[]{:S(2)}, u32[]{:S(2)}) collective-permute-start(bf16[128,768]{1,0:T(8,128)(2,1)S(1)} %get-tuple-element.8), channel_id=1, source_target_pairs={{0,8},{8,16},{16,24},{24,32},{32,40},{40,48},{48,56},{56,64},{64,7... | collective-permute-start | bytes 589832 | tf_op jit(solution)/shard_map/ppermute | solution.py:36
  495.3 1.9 collective-permute-start.4
  498.5 3.8 collective-permute-done.4
  (63 shorter events, 11.0 us)
Async XLA Ops:
  0.6 5.0 copy-start.9
  0.6 5.1 %copy-start.11 = (bf16[12,768]{1,0:T(8,128)(2,1)S(1)}, bf16[12,768]{1,0:T(8,128)(2,1)}, u32[]{:S(2)}) copy-start(bf16[12,768]{1,0:T(8,128)(2,1)} %param.11) | copy-start | bytes 55300
  0.7 5.1 %copy-start.10 = (bf16[12,768]{1,0:T(8,128)(2,1)S(1)}, bf16[12,768]{1,0:T(8,128)(2,1)}, u32[]{:S(2)}) copy-start(bf16[12,768]{1,0:T(8,128)(2,1)} %param.12) | copy-start | bytes 55300
  0.7 13.3 %all-to-all-start.1 = ((bf16[4,1,256,384]{3,2,1,0:T(8,128)(2,1)}), bf16[4,1,256,384]{3,2,1,0:T(8,128)(2,1)S(1)}, u32[]{:S(2)}, u32[]{:S(2)}) async-start(bf16[4,1,256,384]{3,2,1,0:T(8,128)(2,1)} %param.9), calls=%async_computation.1 | async-start | bytes 1572864 | tf_op jit(solution)/shard_map/all_to_all | solution.py:74
  17.6 20.9 %copy-start.6 = (bf16[1,1,256,1536]{3,2,1,0:T(8,128)(2,1)S(1)}, bf16[1,1,256,1536]{3,2,1,0:T(8,128)(2,1)}, u32[]{:S(2)}) copy-start(bf16[1,1,256,1536]{3,2,1,0:T(8,128)(2,1)} %param.8) | copy-start | bytes 2359300
  17.6 28.9 %copy-start.12 = (s32[768]{0:T(1024)S(1)}, s32[768]{0:T(1024)}, u32[]{:S(2)}) copy-start(s32[768]{0:T(1024)} %param.13) | copy-start | bytes 9220
  17.6 398.2 %all-to-all-start = ((bf16[64,12,3840]{2,1,0:T(8,128)(2,1)}), bf16[64,12,3840]{2,1,0:T(8,128)(2,1)}, u32[]{:S(2)}, u32[]{:S(2)}) async-start(bf16[64,12,3840]{2,1,0:T(8,128)(2,1)} %stack.2), calls=%async_computation | async-start | bytes 15728640 | tf_op jit(solution)/shard_map/all_to_all | solution.py:12
  38.6 171.8 %collective-permute-start = (bf16[256,768]{1,0:T(8,128)(2,1)S(1)}, bf16[256,768]{1,0:T(8,128)(2,1)S(1)}, u32[]{:S(2)}, u32[]{:S(2)}) collective-permute-start(bf16[256,768]{1,0:T(8,128)(2,1)S(1)} %slice_bitcast_fusion.9), channel_id=1, source_target_pairs={{0,4},{4,0},{1,5},{5,1},{2,6},{6,2},{3,7},{7,3},{8,12},{12,8},{9,1... | collective-permute-start | bytes 1179656 | tf_op jit(solution)/shard_map/ppermute | solution.py:26
  425.4 2.7 copy-start.1
  425.4 2.7 copy-start.5
  425.4 3.0 copy-start.7
  428.3 3.9 slice-start.2
  428.8 0.7 copy-start.2
  430.3 23.8 %collective-permute-start.2 = (bf16[128,768]{1,0:T(8,128)(2,1)}, bf16[128,768]{1,0:T(8,128)(2,1)}, u32[]{:S(2)}, u32[]{:S(2)}) collective-permute-start(bf16[128,768]{1,0:T(8,128)(2,1)} %get-tuple-element.10), channel_id=1, source_target_pairs={{8,0},{16,8},{24,16},{32,24},{40,32},{48,40},{56,48},{64,56},{72,6... | collective-permute-start | bytes 589832 | tf_op jit(solution)/shard_map/ppermute | solution.py:37
  435.9 20.2 %collective-permute-start.1 = (bf16[128,768]{1,0:T(8,128)(2,1)}, bf16[128,768]{1,0:T(8,128)(2,1)S(1)}, u32[]{:S(2)}, u32[]{:S(2)}) collective-permute-start(bf16[128,768]{1,0:T(8,128)(2,1)} %get-tuple-element.9), channel_id=1, source_target_pairs={{0,8},{8,16},{16,24},{24,32},{32,40},{40,48},{48,56},{56,64},{64,7... | collective-permute-start | bytes 589832 | tf_op jit(solution)/shard_map/ppermute | solution.py:36
  441.3 10.8 %copy-start.3 = (bf16[256,768]{1,0:T(8,128)(2,1)S(1)}, bf16[256,768]{1,0:T(8,128)(2,1)}, u32[]{:S(2)}) copy-start(bf16[256,768]{1,0:T(8,128)(2,1)} %copy-done.2) | copy-start | bytes 1179652
  444.2 34.4 %collective-permute-start.3 = (bf16[256,768]{0,1:T(8,128)(2,1)S(1)}, bf16[256,768]{0,1:T(8,128)(2,1)S(1)}, u32[]{:S(2)}, u32[]{:S(2)}) collective-permute-start(bf16[256,768]{0,1:T(8,128)(2,1)S(1)} %select_bitcast_fusion), channel_id=1, source_target_pairs={{0,4},{4,0},{1,5},{5,1},{2,6},{6,2},{3,7},{7,3},{8,12},{12,8},{9,1... | collective-permute-start | bytes 1179656 | tf_op jit(solution)/shard_map/ppermute | solution.py:26
  452.2 3.9 copy-start
  456.0 1.1 copy-start.8
  456.1 22.7 %slice-start = ((s8[5898240]{0:T(1024)(128)(4,1)}), s8[4194304]{0:T(1024)(128)(4,1)S(1)}, s32[]{:S(2)}) async-start(s8[5898240]{0:T(1024)(128)(4,1)} %bitcast.61), calls=%async_computation.2 | async-start | bytes 8388608
  457.2 21.6 %slice-start.1 = ((s8[5898240]{0:T(1024)(128)(4,1)}), s8[1703936]{0:T(1024)(128)(4,1)S(1)}, s32[]{:S(2)}) async-start(s8[5898240]{0:T(1024)(128)(4,1)} %bitcast.61), calls=%async_computation.3 | async-start | bytes 3407872
  459.4 19.1 %copy-start.4 = (bf16[1,1,256,4,384]{2,4,3,1,0:T(8,128)(2,1)S(1)}, bf16[1,1,256,4,384]{2,4,3,1,0:T(8,128)(2,1)}, u32[]{:S(2)}) copy-start(bf16[1,1,256,4,384]{2,4,3,1,0:T(8,128)(2,1)} %copy.22) | copy-start | bytes 2359300
  479.6 18.3 %collective-permute-start.5 = (bf16[128,768]{1,0:T(8,128)(2,1)S(1)}, bf16[128,768]{1,0:T(8,128)(2,1)S(1)}, u32[]{:S(2)}, u32[]{:S(2)}) collective-permute-start(bf16[128,768]{1,0:T(8,128)(2,1)S(1)} %get-tuple-element.8), channel_id=1, source_target_pairs={{0,8},{8,16},{16,24},{24,32},{32,40},{40,48},{48,56},{56,64},{64,7... | collective-permute-start | bytes 589832 | tf_op jit(solution)/shard_map/ppermute | solution.py:36
  495.3 7.0 %collective-permute-start.4 = (bf16[128,768]{1,0:T(8,128)(2,1)S(1)}, bf16[128,768]{1,0:T(8,128)(2,1)S(1)}, u32[]{:S(2)}, u32[]{:S(2)}) collective-permute-start(bf16[128,768]{1,0:T(8,128)(2,1)S(1)} %get-tuple-element.7), channel_id=1, source_target_pairs={{8,0},{16,8},{24,16},{32,24},{40,32},{48,40},{56,48},{64,56},{72,6... | collective-permute-start | bytes 589832 | tf_op jit(solution)/shard_map/ppermute | solution.py:37
